TPU v7x, 768 devices: a whole 4x8x12 slice. The times are simulated.
768 devices in a mesh: batch: 8 (over y), row: 8 (over z_lo, core), col: 12 (over x, z_hi).
Axes of the slice: x: 4, y: 8, z: 12 (z_hi: 3, z_lo: 4; z = z_hi * 4 + z_lo), core: 2. Of those that a mesh axis runs over, the one named last changes fastest.
Arguments:
- tokens: bfloat16 [4096, 6144], P('batch', 'row'), may hold values from -6 to 6
- cotangent: bfloat16 [4096, 6144], P('batch', 'row'), may hold values from -1.5 to 1.5
- weight_in: bfloat16 [6144, 12288], P('row', 'col'), may hold values from -0.078125 to 0.078125
- weight_out: bfloat16 [12288, 6144], P('col', 'row'), may hold values from -0.0546875 to 0.0546875
- segment_ids: int32 [4096], P('batch'), may hold values from 0 to 31, as said below
- keep_mask: int32 [4096], P('batch'), may hold values 0 or 1
Outputs:
- grad_tokens: bfloat16 [4096, 6144], P('batch', 'row')
- grad_weight_in: bfloat16 [6144, 12288], P(('row', 'batch'), 'col')
- grad_weight_out: bfloat16 [12288, 6144], P('col', ('row', 'batch'))
Inputs may be any that keep to these rules, and one draw needn't show every extreme that they name: `segment_ids`: never falling along the bin; every image 0 .. 31 has 1 to 192 tokens, and some image has exactly 192.
All inputs are finite; a program needn't handle non-finite values. No bound on the sum of `keep_mask` on one device may be relied on, other than what follows from the above.
Results may differ from a plain program's by a relative error of at most 0.023.
Values may be sent and summed in bfloat16 or wider, within the bound.
A program may use at most 32 MiB of HBM per device.

v0:
```python
import jax
import jax.numpy as jnp
from jax import lax
from jax.sharding import PartitionSpec as P

SEGS = 32
IMAGE_MEAN = 128


inv_root_two = 0.7071067811865476
inv_root_tau = 0.3989422804014327


def padded(x, sides, width):
    for axis, dim in sides:
        size, length = (lax.axis_size(axis), x.shape[dim])
        up = [(i, (i + 1) % size) for i in range(size - 1)]
        down = [(j, i) for i, j in up]
        last = lax.slice_in_dim(x, length - width, length, axis=dim)
        first = lax.slice_in_dim(x, 0, width, axis=dim)
        before = lax.ppermute(last, axis, up)
        after = lax.ppermute(first, axis, down)
        x = jnp.concatenate([before, x, after], axis=dim)
    return x


def gelu_parts(pre_act):
    normal_cdf = 0.5 * (1.0 + lax.erf(pre_act * inv_root_two))
    slopes = normal_cdf + pre_act * jnp.exp(-0.5 * pre_act * pre_act) * inv_root_tau
    return (pre_act * normal_cdf, slopes)


def contract_cols(left, right):
    return lax.dot_general(
        left, right, (((1,), (1,)), ((), ())), preferred_element_type=jnp.float32
    )


def contract_rows(left, right):
    return lax.dot_general(
        left, right, (((0,), (0,)), ((), ())), preferred_element_type=jnp.float32
    )


def per_device(tokens, cotangent, weight_in, weight_out, segment_ids, keep_mask):
    labels = jnp.arange(SEGS, dtype=jnp.int32)
    onehot = (segment_ids[:, None] == labels[None, :]).astype(jnp.float32)
    keeping = keep_mask.astype(jnp.float32)
    local_sizes = jnp.sum(onehot * keeping[:, None], axis=0)
    beside = padded(local_sizes[None, :], (("batch", 0),), 1)
    image_sizes = jnp.sum(beside, axis=0)
    per_token = jnp.dot(onehot, image_sizes, precision=lax.Precision.HIGHEST)
    token_weight = keeping * jnp.sqrt(IMAGE_MEAN / jnp.maximum(per_token, 1.0))
    scaled = (cotangent.astype(jnp.float32) * token_weight[:, None]).astype(jnp.bfloat16)
    hidden_cols = weight_in.shape[1]
    forward_part = jnp.dot(tokens, weight_in, preferred_element_type=jnp.float32)
    backward_part = contract_cols(scaled, weight_out)
    pre_act, back_grad = (
        lax.psum(forward_part.astype(jnp.bfloat16), "row").astype(jnp.float32),
        lax.psum(backward_part.astype(jnp.bfloat16), "row").astype(jnp.float32),
    )
    activation, slopes = gelu_parts(pre_act)
    activation = activation.astype(jnp.bfloat16)
    hidden_grad = (back_grad * slopes).astype(jnp.bfloat16)
    input_part = contract_cols(hidden_grad, weight_in)
    grad_tokens = lax.psum(input_part.astype(jnp.bfloat16), "col")
    first_grad = contract_rows(tokens, hidden_grad)
    second_grad = contract_rows(scaled, activation)
    summed_grads = lax.psum_scatter(
        jnp.concatenate([first_grad, second_grad], axis=1).astype(jnp.bfloat16),
        "batch",
        scatter_dimension=0,
        tiled=True,
    ).astype(jnp.float32)
    grad_in = summed_grads[:, :hidden_cols].astype(jnp.bfloat16)
    grad_out = summed_grads[:, hidden_cols:].T.astype(jnp.bfloat16)
    return (grad_tokens, grad_in, grad_out)


def solution(mesh):
    return jax.shard_map(
        per_device,
        mesh=mesh,
        in_specs=(
            P("batch", "row"),
            P("batch", "row"),
            P("row", "col"),
            P("col", "row"),
            P("batch"),
            P("batch"),
        ),
        out_specs=(P("batch", "row"), P(("row", "batch"), "col"), P("col", ("row", "batch"))),
        check_vma=False,
    )
```

profile of v0, /device:TPU:8, one launch (start us, length us, event | category | flops | bytes accessed | tf_op | source)
XLA Modules:
  0.0 363.1 jit_solution(9273533914684698217)
XLA Ops:
  7.2 0.0 copy-start
  7.2 0.0 all-reduce.6.cloned.1.call-start
  7.2 0.8 convert_element_type.39
  8.0 0.8 select_reduce_fusion
  8.8 0.0 copy-start.3
  8.8 0.0 copy-start.5
  8.8 0.0 copy-start.6
  8.9 11.5 %collective-permute-start.1 = (f32[1,32]{1,0:T(1,128)S(1)}, f32[1,32]{1,0:T(1,128)S(1)}, u32[]{:S(2)}, u32[]{:S(2)}) collective-permute-start(f32[1,32]{1,0:T(1,128)S(1)} %bitcast.29), channel_id=1, source_target_pairs={{96,0},{192,96},{288,192},{384,288},{480,384},{576,480},{672,576},... | collective-permute-start | bytes 392 | tf_op jit(solution)/shard_map/ppermute | solution.py:22
  20.3 1.9 collective-permute-start
  22.3 3.1 convolution_convert_fusion.2
  25.4 0.0 collective-permute-done.1
  25.4 0.4 collective-permute-done
  25.8 0.1 fusion.11
  26.0 2.0 convolution_convert_fusion.3
  28.0 0.0 all-reduce.6.cloned.1.call-update
  28.0 0.0 reduce-scatter.4.cloned.1.call-start
  28.1 90.1 %all-reduce.6.cloned.1.call-done = (bf16[512,1024]{1,0:T(8,128)(2,1)}, bf16[512,1024]{1,0:T(8,128)(2,1)}) async-done(((bf16[512,1024]{1,0:T(8,128)(2,1)}, bf16[512,1024]{1,0:T(8,128)(2,1)}), (bf16[512,1024]{1,0:T(8,128)(2,1)}, bf16[512,1024]{1,0:T(8,128)(2,1)})) %all-reduce.6.cloned.1.call-update) | async-done | bytes 2097168 | tf_op jit(solution)/shard_map/psum | solution.py:59
  118.2 2.6 convolution_convert_fusion
  120.8 0.0 copy-start.7
  120.9 1.0 fusion.7
  121.9 0.1 copy-done.7
  122.0 1.0 fusion.9
  123.0 1.9 pad_maximum_fusion
  124.9 4.7 %copy.19 = bf16[768,2048]{1,0:T(8,128)(2,1)} copy(bf16[768,2048]{0,1:T(8,128)(2,1)} %pad_maximum_fusion) | data formatting | bytes 6291456
  129.6 0.0 reduce-scatter.4.cloned.1.call-update
  129.6 0.0 all-reduce.4.cloned.1.call-start
  129.6 1.9 convolution_convert_fusion.4
  131.5 0.0 all-reduce.4.cloned.1.call-update
  131.6 49.2 %reduce-scatter.4.cloned.1.call-done = bf16[96,2048]{1,0:T(8,128)(2,1)} async-done(((bf16[768,2048]{1,0:T(8,128)(2,1)}), bf16[96,2048]{1,0:T(8,128)(2,1)}) %reduce-scatter.4.cloned.1.call-update) | async-done | bytes 393232
  180.8 1.8 slice_bitcast_fusion
  182.6 171.9 %all-reduce.4.cloned.1.call-done = bf16[512,768]{1,0:T(8,128)(2,1)} async-done(((bf16[512,768]{1,0:T(8,128)(2,1)}), bf16[512,768]{1,0:T(8,128)(2,1)}) %all-reduce.4.cloned.1.call-update) | async-done | bytes 786448 | tf_op jit(solution)/shard_map/psum | solution.py:66
  354.5 2.1 copy.27
  (11 shorter events, 0.0 us)
Async XLA Ops:
  7.2 15.1 %copy-start = (bf16[768,1024]{1,0:T(8,128)(2,1)S(1)}, bf16[768,1024]{1,0:T(8,128)(2,1)}, u32[]{:S(2)}) copy-start(bf16[768,1024]{1,0:T(8,128)(2,1)} %param.8) | copy-start | bytes 4718596
  7.2 111.0 %all-reduce.6.cloned.1.call-start = ((), (), s32[]{:S(2)}) async-start(), calls=%async_computation.3 | async-start | bytes 4194304 | tf_op jit(solution)/shard_map/psum | solution.py:59
  8.8 17.0 %copy-start.4 = (s32[512]{0:T(512)S(1)}, s32[512]{0:T(512)}, u32[]{:S(2)}) copy-start(s32[512]{0:T(512)} %param.10) | copy-start | bytes 6148
  8.8 17.1 %copy-start.3 = (s32[512]{0:T(512)S(1)}, s32[512]{0:T(512)}, u32[]{:S(2)}) copy-start(s32[512]{0:T(512)} %param.11) | copy-start | bytes 6148
  8.8 17.1 %copy-start.5 = (bf16[1024,768]{1,0:T(8,128)(2,1)S(1)}, bf16[1024,768]{1,0:T(8,128)(2,1)}, u32[]{:S(2)}) copy-start(bf16[1024,768]{1,0:T(8,128)(2,1)} %param.9) | copy-start | bytes 4718596
  8.8 17.1 %copy-start.6 = (bf16[512,768]{1,0:T(8,128)(2,1)S(1)}, bf16[512,768]{1,0:T(8,128)(2,1)}, u32[]{:S(2)}) copy-start(bf16[512,768]{1,0:T(8,128)(2,1)} %param.7) | copy-start | bytes 2359300
  8.9 16.5 %collective-permute-start.1 = (f32[1,32]{1,0:T(1,128)S(1)}, f32[1,32]{1,0:T(1,128)S(1)}, u32[]{:S(2)}, u32[]{:S(2)}) collective-permute-start(f32[1,32]{1,0:T(1,128)S(1)} %bitcast.29), channel_id=1, source_target_pairs={{96,0},{192,96},{288,192},{384,288},{480,384},{576,480},{672,576},... | collective-permute-start | bytes 392 | tf_op jit(solution)/shard_map/ppermute | solution.py:22
  20.3 5.5 %collective-permute-start = (f32[1,32]{1,0:T(1,128)S(1)}, f32[1,32]{1,0:T(1,128)S(1)}, u32[]{:S(2)}, u32[]{:S(2)}) collective-permute-start(f32[1,32]{1,0:T(1,128)S(1)} %bitcast.30), channel_id=1, source_target_pairs={{0,96},{96,192},{192,288},{288,384},{384,480},{480,576},{576,672},... | collective-permute-start | bytes 392 | tf_op jit(solution)/shard_map/ppermute | solution.py:21
  28.0 152.8 %reduce-scatter.4.cloned.1.call-start = ((), (), s32[]{:S(2)}) async-start(), calls=%async_computation.2 | async-start | bytes 3538944
  118.2 2.6 copy-start.1
  118.2 2.6 copy-start.2
  120.8 1.1 copy-start.7
  129.6 224.9 %all-reduce.4.cloned.1.call-start = ((), (), s32[]{:S(2)}) async-start(), calls=%async_computation.1 | async-start | bytes 1572864 | tf_op jit(solution)/shard_map/psum | solution.py:66
Sparse Core Ops, SparseCore 0:
  28.2 90.0 all-reduce.5
  129.7 51.0 reduce-scatter.3
  184.6 169.8 all-reduce.3
where the time goes:
time: 363 us
  waiting for transfers between devices  312 us (86%)
  between operations  13.9 us (4%)
  starting transfers between devices  13.5 us (4%)
  matrix products  10.8 us (3%)
  local copies, waits for them, and re-layouts  8.62 us (2%)
  other arithmetic  4.53 us (1%)
    psum x1, waiting for transfers between devices, per_device(): grad_tokens = lax.psum(input_part.astype(jnp.bfloat16), 'col')  172 us
    psum x1, waiting for transfers between devices, per_device(): lax.psum(forward_part.astype(jnp.bfloat16), 'row').astype(jnp.float32)  90.1 us
    unnamed x4, waiting for transfers between devices  49.3 us
    ppermute x1, starting transfers between devices, padded(): after = lax.ppermute(first, axis, down)  11.5 us
  transfers between devices with their start and end apart: 5, of which 4 were waited for; matrix products, arithmetic and copies ran while one was open for 2% of the time, Pallas kernels for 0%

commit v1 on v0

v1 whole, which is shorter than its diff:
```python
import functools

import jax
import jax.numpy as jnp
from jax import lax
from jax.experimental import pallas as pl
from jax.experimental.pallas import tpu as pltpu
from jax.sharding import PartitionSpec as P

SEGS = 32
IMAGE_MEAN = 128.0
MESH = pl.DeviceIdType.MESH

inv_root_two = 0.7071067811865476
inv_root_tau = 0.3989422804014327

F32 = jnp.float32
BF16 = jnp.bfloat16


def dot(left, right, lc, rc):
    return lax.dot_general(
        left, right, (((lc,), (rc,)), ((), ())), preferred_element_type=F32
    )


def gelu_parts(pre_act):
    normal_cdf = 0.5 * (1.0 + lax.erf(pre_act * inv_root_two))
    slopes = normal_cdf + pre_act * jnp.exp(-0.5 * pre_act * pre_act) * inv_root_tau
    return (pre_act * normal_cdf, slopes)


def remote(src, dst, send, recv, where):
    return pltpu.make_async_remote_copy(
        src_ref=src,
        dst_ref=dst,
        send_sem=send,
        recv_sem=recv,
        device_id=where,
        device_id_type=MESH,
    )


CHUNKS = 16
GROUPS = 2
PER = CHUNKS // GROUPS


def row_kernel(
    tokens_h, cotangent_h, w_in_h, w_out_h, hid_out,
    tokens, cotangent, w_in, w_out, snd, prt, acc, rcv, run, hid,
    pair_s, pair_r, sum_s, sum_r, back_s, back_r, side_s, side_r, out_sem, in_sem,
):
    row = lax.axis_index("row")
    core = row % 2
    z = row // 2
    place = core * z + (1 - core) * (3 - z)
    step = 4 * core - 2
    ahead = {"row": (row + step + 8) % 8}
    behind = {"row": (row - step + 8) % 8}
    partner = {"row": row + 1 - 2 * core}
    half = acc.shape[3]
    rows = acc.shape[2]
    block = PER * rows

    barrier = pltpu.get_barrier_semaphore()
    for where in (partner, ahead, behind):
        pl.semaphore_signal(barrier, inc=1, device_id=where, device_id_type=MESH)

    def columns(which):
        return pl.ds(pl.multiple_of(which * half, half), half)

    other = columns(1 - core)
    mine = columns(core)
    loads = [
        pltpu.make_async_copy(src, dst, in_sem.at[i])
        for i, (src, dst) in enumerate((
            (tokens_h, tokens),
            (w_in_h.at[:, other], w_in.at[:, other]),
            (cotangent_h, cotangent),
            (w_out_h.at[other, :], w_out.at[other, :]),
            (w_in_h.at[:, mine], w_in.at[:, mine]),
            (w_out_h.at[mine, :], w_out.at[mine, :]),
        ))
    ]
    for load in loads:
        load.start()

    def pair(g):
        part = pl.ds(g * PER, PER)
        return remote(snd.at[part], prt.at[part], pair_s.at[g], pair_r.at[g], partner)

    def products(cols, g, into, waits=()):
        toks = pl.ds(g * block, block)
        part = pl.ds(g * PER, PER)
        for i in waits[:-1]:
            loads[i].wait()
        fwd = dot(tokens[toks, :], w_in[:, cols], 1, 0)
        into[part, 0] = fwd.reshape(PER, rows, half).astype(into.dtype)
        if waits:
            loads[waits[-1]].wait()
        bwd = dot(cotangent[toks, :], w_out[cols, :], 1, 1)
        into[part, 1] = bwd.reshape(PER, rows, half).astype(into.dtype)

    loads[2].wait()
    products(other, 0, snd, (0, 1, 3))
    pl.semaphore_wait(barrier, 3)
    pair(0).start()
    products(other, 1, snd)
    pair(1).start()
    products(mine, 0, acc, (4, 5))
    products(mine, 1, acc)

    def onward(j):
        return remote(run.at[j], rcv.at[j], sum_s.at[j], sum_r.at[j], ahead)

    def back(j):
        spot = hid.at[core, j]
        return remote(spot, spot, back_s.at[j], back_r.at[j], behind)

    def side(j, which):
        spot = hid.at[which, j]
        return remote(spot, spot, side_s.at[j], side_r.at[j], partner)

    def save(j, which):
        return pltpu.make_async_copy(
            hid.at[which, j], hid_out.at[which, j], out_sem.at[which, j]
        )

    for g in range(GROUPS):
        pair(g).wait_recv()

        @pl.when(place == 0)
        def _():
            @pl.loop(g * PER, (g + 1) * PER)
            def _(j):
                run[j] = (acc[j] + prt[j].astype(F32)).astype(BF16)
                onward(j).start()

        @pl.when((place > 0) & (place < 3))
        def _():
            @pl.loop(g * PER, (g + 1) * PER)
            def _(j):
                own = acc[j] + prt[j].astype(F32)
                onward(j).wait_recv()
                run[j] = (own + rcv[j].astype(F32)).astype(BF16)
                onward(j).start()

        @pl.when(place == 3)
        def _():
            @pl.loop(g * PER, (g + 1) * PER)
            def _(j):
                onward(j).wait_recv()
                pre = acc[j, 0] + prt[j, 0].astype(F32) + rcv[j, 0].astype(F32)
                grad = acc[j, 1] + prt[j, 1].astype(F32) + rcv[j, 1].astype(F32)
                act, slopes = gelu_parts(pre)
                hid[core, j, 0] = act.astype(BF16)
                hid[core, j, 1] = (grad * slopes).astype(BF16)
                back(j).start()
                side(j, core).start()
                save(j, core).start()

    @pl.when(place < 3)
    def _():
        @pl.loop(0, CHUNKS)
        def _(j):
            back(j).wait_recv()

            @pl.when(place > 0)
            def _():
                back(j).start()

            side(j, core).start()
            save(j, core).start()

    @pl.loop(0, CHUNKS)
    def _(j):
        side(j, 1 - core).wait_recv()
        save(j, 1 - core).start()

    for g in range(GROUPS):
        pair(g).wait_send()

    @pl.loop(0, CHUNKS)
    def _(j):
        side(j, core).wait_send()
        save(j, 0).wait()
        save(j, 1).wait()

    @pl.when(place < 3)
    def _():
        @pl.loop(0, CHUNKS)
        def _(j):
            onward(j).wait_send()

    @pl.when(place > 0)
    def _():
        @pl.loop(0, CHUNKS)
        def _(j):
            back(j).wait_send()


def row_stage(tokens, cotangent, w_in, w_out):
    toks, width = tokens.shape
    cols = w_in.shape[1]
    half = cols // 2
    rows = toks // CHUNKS
    slab = (CHUNKS, 2, rows, half)
    dma = pltpu.SemaphoreType.DMA
    return pl.pallas_call(
        row_kernel,
        out_shape=jax.ShapeDtypeStruct((2,) + slab, BF16),
        in_specs=[pl.BlockSpec(memory_space=pltpu.MemorySpace.HBM)] * 4,
        out_specs=pl.BlockSpec(memory_space=pl.ANY),
        scratch_shapes=[
            pltpu.VMEM((toks, width), BF16),
            pltpu.VMEM((toks, width), BF16),
            pltpu.VMEM((width, cols), BF16),
            pltpu.VMEM((cols, width), BF16),
            pltpu.VMEM(slab, BF16),
            pltpu.VMEM(slab, BF16),
            pltpu.VMEM(slab, F32),
            pltpu.VMEM(slab, BF16),
            pltpu.VMEM(slab, BF16),
            pltpu.VMEM((2,) + slab, BF16),
            dma((GROUPS,)), dma((GROUPS,)),
            dma((CHUNKS,)), dma((CHUNKS,)),
            dma((CHUNKS,)), dma((CHUNKS,)),
            dma((CHUNKS,)), dma((CHUNKS,)),
            dma((2, CHUNKS)),
            dma((6,)),
        ],
        compiler_params=pltpu.CompilerParams(
            collective_id=0, has_side_effects=True, vmem_limit_bytes=32 << 20
        ),
        cost_estimate=pl.CostEstimate(
            flops=4 * toks * width * cols, bytes_accessed=40 << 20, transcendentals=0
        ),
        name="row_stage",
    )(tokens, cotangent, w_in, w_out)


def grad_kernel(
    n_batch, n_x, n_z,
    hid, tokens, cotangent, w_in, seg, keep,
    g_tok, g_in, g_out,
    weighted, grads, y_first, y_rest, part, x_first, x_last, z_send, z_recv, total,
    counts, counts_in,
    count_s, count_r, y_s, y_r, x_s, x_r, z_s, z_r, zg_s, zg_r, xg_s, xg_r, out_sem,
):
    b = lax.axis_index("batch")
    col = lax.axis_index("col")
    xi = col // n_z
    q = col % n_z
    half = hid.shape[4]
    toks = tokens.shape[0]
    third = part.shape[2]
    piece = grads.shape[2]
    split = piece // 2
    own_rows = toks // n_x
    own_half = own_rows // 2
    own_split = own_half // 2

    y_next = {"batch": (b + 1) % n_batch}
    y_prev = {"batch": (b + n_batch - 1) % n_batch}
    x_next = {"col": ((xi + 1) % n_x) * n_z + q}
    x_prev = {"col": ((xi + n_x - 1) % n_x) * n_z + q}
    z_one = {"col": xi * n_z + (q + 1) % n_z}
    z_two = {"col": xi * n_z + (q + 2) % n_z}
    y_to = (y_next, y_prev)
    x_to = (x_next, x_prev)
    z_to = (z_one, z_two)

    barrier = pltpu.get_barrier_semaphore()
    for where in y_to + x_to + z_to:
        pl.semaphore_signal(barrier, inc=1, device_id=where, device_id_type=MESH)

    labels = lax.broadcasted_iota(jnp.int32, (SEGS, toks), 0)
    marks = jnp.where((labels == seg[...]) & (keep[...] == 1), 1.0, 0.0).astype(F32)
    counts[...] = jnp.broadcast_to(
        jnp.sum(marks, axis=1, keepdims=True), counts.shape
    )
    pl.semaphore_wait(barrier, 6)

    def count_copy(d):
        return remote(counts, counts_in.at[d], count_s.at[d], count_r.at[d], y_to[d])

    count_copy(0).start()
    count_copy(1).start()

    def hidden(h, a):
        return hid[h, :, a].reshape(toks, half)

    raw = []
    for i in range(3):
        rows = pl.ds(i * third, third)
        raw.append(
            dot(hidden(0, 1), w_in[rows, 0:half], 1, 1)
            + dot(hidden(1, 1), w_in[rows, half:2 * half], 1, 1)
        )
    count_copy(0).wait_recv()
    count_copy(1).wait_recv()
    sizes = counts[...] + counts_in[0] + counts_in[1]
    sizes = jnp.concatenate([sizes, sizes], axis=1)
    per_token = dot(marks, sizes, 0, 0)
    weight = jnp.where(
        per_token > 0.0, jnp.sqrt(IMAGE_MEAN / jnp.maximum(per_token, 1.0)), 0.0
    )
    for i in range(3):
        part[i] = (raw[i] * weight).astype(BF16)

    def rows_of(ref, owner, start, size):
        first = pl.multiple_of(owner * own_rows + start, size)
        return ref.at[:, pl.ds(first, size), :]

    x_far = (xi + 2) % n_x
    x_near = ((xi + 1) % n_x, (xi + n_x - 1) % n_x)

    def x_sum(u, s, d):
        start = u * own_half
        if s == 0:
            src = rows_of(part, x_far, start + d * own_split, own_split)
            dst = x_first.at[u, d]
        else:
            src = rows_of(part, x_near[d], start, own_half)
            dst = x_last.at[u, d]
        return remote(src, dst, x_s.at[u, s, d], x_r.at[u, s, d], x_to[d])

    for u in range(2):
        x_sum(u, 0, 0).start()
        x_sum(u, 0, 1).start()

    def y_owner(s, d):
        shift = 4 - s
        return (b + shift) % n_batch if d == 0 else (b + n_batch - shift) % n_batch

    def y_sum(a, s, d):
        src = grads.at[a, y_owner(s, d)]
        if s == 0:
            src = src.at[pl.ds(d * split, split), :]
            dst = y_first.at[a, d]
        else:
            dst = y_rest.at[a, d, s - 1]
        return remote(src, dst, y_s.at[a, s, d], y_r.at[a, s, d], y_to[d])

    def products(a, source):
        for i in range(3):
            lanes = pl.ds(i * third, third)
            weighted[:, lanes] = (source[:, lanes].astype(F32) * weight).astype(BF16)
        for h in range(2):
            block = dot(weighted[...], hidden(h, 1 - a), 0, 0)
            grads[a, :, :, h * half:(h + 1) * half] = block.reshape(
                n_batch, piece, half
            ).astype(BF16)
        y_sum(a, 0, 0).start()
        y_sum(a, 0, 1).start()

    def y_onward(a, s):
        for d in range(2):
            y_sum(a, s - 1, d).wait_recv()
            owner = y_owner(s, d)
            if s == 1:
                lines = pl.ds(d * split, split)
                grads[a, owner, lines, :] = (
                    grads[a, owner, lines, :].astype(F32) + y_first[a, d].astype(F32)
                ).astype(BF16)
            else:
                grads[a, owner] = (
                    grads[a, owner].astype(F32) + y_rest[a, d, s - 2].astype(F32)
                ).astype(BF16)
            y_sum(a, s, d).start()

    def y_finish(a, out):
        y_sum(a, 3, 0).wait_recv()
        y_sum(a, 3, 1).wait_recv()
        out[...] = (
            grads[a, b].astype(F32)
            + y_rest[a, 0, 2].astype(F32)
            + y_rest[a, 1, 2].astype(F32)
        ).astype(BF16)

    def x_onward(u):
        for d in range(2):
            x_sum(u, 0, d).wait_recv()
            first = x_near[d] * own_rows + u * own_half + d * own_split
            lines = pl.ds(pl.multiple_of(first, own_split), own_split)
            part[:, lines, :] = (
                part[:, lines, :].astype(F32) + x_first[u, d].astype(F32)
            ).astype(BF16)
            x_sum(u, 1, d).start()

    def z_sum(u, k):
        target = (q + 1 + k) % n_z
        return remote(
            z_send.at[u, target], z_recv.at[u, k], z_s.at[u, k], z_r.at[u, k], z_to[k]
        )

    def mine(u):
        return pl.ds(pl.multiple_of(xi * own_rows + u * own_half, own_half), own_half)

    def z_scatter(u):
        x_sum(u, 1, 0).wait_recv()
        x_sum(u, 1, 1).wait_recv()
        z_send[u] = (
            part[:, mine(u), :].astype(F32)
            + x_last[u, 0].astype(F32)
            + x_last[u, 1].astype(F32)
        ).astype(BF16)
        z_sum(u, 0).start()
        z_sum(u, 1).start()

    def z_give(u, k):
        spot = total.at[q, mine(u), :]
        return remote(spot, spot, zg_s.at[u, k], zg_r.at[u, k], z_to[k])

    def z_gather(u):
        z_sum(u, 0).wait_recv()
        z_sum(u, 1).wait_recv()
        total[q, mine(u), :] = (
            z_send[u, q].astype(F32)
            + z_recv[u, 0].astype(F32)
            + z_recv[u, 1].astype(F32)
        ).astype(BF16)
        z_give(u, 0).start()
        z_give(u, 1).start()

    def x_give(u, s, d):
        start = u * own_half
        if s == 0:
            spot = rows_of(total, xi, start, own_half)
        else:
            spot = rows_of(total, x_near[1 - d], start + d * own_split, own_split)
        return remote(spot, spot, xg_s.at[u, s, d], xg_r.at[u, s, d], x_to[d])

    def x_gather(u):
        z_give(u, 0).wait_recv()
        z_give(u, 1).wait_recv()
        x_give(u, 0, 0).start()
        x_give(u, 0, 1).start()

    def x_forward(u):
        for d in range(2):
            x_give(u, 0, d).wait_recv()
            x_give(u, 1, d).start()

    def save(i):
        return pltpu.make_async_copy(
            total.at[i], g_tok.at[:, pl.ds(i * third, third)], out_sem.at[i]
        )

    products(1, cotangent)
    x_onward(0)
    x_onward(1)
    products(0, tokens)
    z_scatter(0)
    y_onward(1, 1)
    z_scatter(1)
    y_onward(0, 1)
    z_gather(0)
    y_onward(1, 2)
    z_gather(1)
    y_onward(0, 2)
    x_gather(0)
    y_onward(1, 3)
    x_gather(1)
    x_forward(0)
    y_onward(0, 3)
    x_forward(1)
    y_finish(1, g_out)
    for u in range(2):
        x_give(u, 1, 0).wait_recv()
        x_give(u, 1, 1).wait_recv()
    for i in range(3):
        save(i).start()
    y_finish(0, g_in)

    for d in range(2):
        count_copy(d).wait_send()
        for u in range(2):
            z_sum(u, d).wait_send()
            z_give(u, d).wait_send()
            for s in range(2):
                x_sum(u, s, d).wait_send()
                x_give(u, s, d).wait_send()
        for s in range(4):
            for a in range(2):
                y_sum(a, s, d).wait_send()
    for i in range(3):
        save(i).wait()


def grad_stage(mesh_shape, hid, tokens, cotangent, w_in, seg, keep):
    n_batch = mesh_shape["batch"]
    n_x, n_z = 4, mesh_shape["col"] // 4
    toks, width = tokens.shape
    cols = w_in.shape[1]
    third = width // 3
    piece = width // n_batch
    own = toks // n_x
    dma = pltpu.SemaphoreType.DMA
    vmem = pl.BlockSpec(memory_space=pltpu.VMEM)
    return pl.pallas_call(
        functools.partial(grad_kernel, n_batch, n_x, n_z),
        out_shape=(
            jax.ShapeDtypeStruct((toks, width), BF16),
            jax.ShapeDtypeStruct((piece, cols), BF16),
            jax.ShapeDtypeStruct((piece, cols), BF16),
        ),
        in_specs=[vmem] * 6,
        out_specs=(pl.BlockSpec(memory_space=pl.ANY), vmem, vmem),
        scratch_shapes=[
            pltpu.VMEM((toks, width), BF16),
            pltpu.VMEM((2, n_batch, piece, cols), BF16),
            pltpu.VMEM((2, 2, piece // 2, cols), BF16),
            pltpu.VMEM((2, 2, 3, piece, cols), BF16),
            pltpu.VMEM((3, toks, third), BF16),
            pltpu.VMEM((2, 2, 3, own // 4, third), BF16),
            pltpu.VMEM((2, 2, 3, own // 2, third), BF16),
            pltpu.VMEM((2, 3, own // 2, third), BF16),
            pltpu.VMEM((2, 2, own // 2, third), BF16),
            pltpu.VMEM((3, toks, third), BF16),
            pltpu.VMEM((SEGS, 128), F32),
            pltpu.VMEM((2, SEGS, 128), F32),
            dma((2,)), dma((2,)),
            dma((2, 4, 2)), dma((2, 4, 2)),
            dma((2, 2, 2)), dma((2, 2, 2)),
            dma((2, 2)), dma((2, 2)),
            dma((2, 2)), dma((2, 2)),
            dma((2, 2, 2)), dma((2, 2, 2)),
            dma((3,)),
        ],
        compiler_params=pltpu.CompilerParams(
            collective_id=1, has_side_effects=True, vmem_limit_bytes=40 << 20
        ),
        cost_estimate=pl.CostEstimate(
            flops=6 * toks * width * cols, bytes_accessed=40 << 20, transcendentals=0
        ),
        name="grad_stage",
    )(hid, tokens, cotangent, w_in, seg, keep)


def per_device(mesh_shape, tokens, cotangent, weight_in, weight_out, segment_ids, keep_mask):
    hid = row_stage(*(
        pltpu.with_memory_space_constraint(x, pltpu.MemorySpace.HBM)
        for x in (tokens, cotangent, weight_in, weight_out)
    ))
    grad_tokens, grad_in, grad_out = grad_stage(
        mesh_shape, hid, tokens, cotangent, weight_in,
        segment_ids[None, :], keep_mask[None, :],
    )
    return (grad_tokens, grad_in, grad_out.T)


def solution(mesh):
    return jax.shard_map(
        functools.partial(per_device, dict(mesh.shape)),
        mesh=mesh,
        in_specs=(
            P("batch", "row"),
            P("batch", "row"),
            P("row", "col"),
            P("col", "row"),
            P("batch"),
            P("batch"),
        ),
        out_specs=(P("batch", "row"), P(("row", "batch"), "col"), P("col", ("row", "batch"))),
        check_vma=False,
    )
```

time: 363 us -> 104 us (0.29)
  the two profiles are of different devices: /device:TPU:8 before, /device:TPU:192 now
where the time goes in v1:
time: 104 us
  Pallas kernels  101 us (97%)
  local copies, waits for them, and re-layouts  2.26 us (2%)
    pallas_call x1, Pallas kernels, grad_stage(): pl.pallas_call(functools.partial(grad_kernel, n_batch, n_x, n_z), out_sha...  50.5 us
    pallas_call x1, Pallas kernels, row_stage(): pl.pallas_call(row_kernel, out_shape=jax.ShapeDtypeStruct((2,) + slab, BF...  50.3 us
    unnamed x13, local copies, waits for them, and re-layouts  2.26 us

profile of v1, /device:TPU:192, one launch (start us, length us, event | category | flops | bytes accessed | tf_op | source)
XLA Modules:
  0.0 103.7 jit_solution(1051518675962325755)
XLA Ops:
  0.6 0.0 copy-start
  0.6 0.0 copy-start.1
  0.7 0.0 copy-start.2
  0.7 0.0 copy-start.3
  0.7 0.0 copy-start.4
  0.7 50.3 %row_stage.1.hid = bf16[2,16,2,32,512]{4,3,2,1,0:T(8,128)(2,1)S(1)} custom-call(bf16[512,768]{1,0:T(8,128)(2,1)} %tokens.1, bf16[512,768]{1,0:T(8,128)(2,1)} %cotangent.1, bf16[768,1024]{1,0:T(8,128)(2,1)} %w_in.1, bf16[1024,768]{1,0:T(8,128)(2,1)} %w_out_h.1), custom_call_target="tpu_custom_call" | custom-call | flops 1610612736 | bytes 41943040 | tf_op jit(solution)/shard_map/row_stage/pallas_call | solution.py:210
  50.9 0.0 copy-done
  51.0 0.0 copy-done.1
  51.0 0.0 copy-done.2
  51.0 0.0 copy-done.3
  51.0 0.0 copy-done.4
  51.0 50.5 %grad_stage.1 = (bf16[512,768]{1,0:T(8,128)(2,1)S(1)}, bf16[96,1024]{1,0:T(8,128)(2,1)S(1)}, bf16[96,1024]{1,0:T(8,128)(2,1)S(1)}) custom-call(bf16[2,16,2,32,512]{4,3,2,1,0:T(8,128)(2,1)S(1)} %row_stage.1.hid, bf16[512,768]{1,0:T(8,128)(2,1)S(1)} %copy-done.1, bf16[512,768]{1,0:T(8,128)(2,1)S(1)} %copy-done.2, bf16[768,1024]{1,0:T(8,128)(2,1)S(1)} %copy-done, ...), custom_call_target="tpu_custom_call" | custom-call | flops 2415919104 | bytes 41943040 | tf_op jit(solution)/shard_map/grad_stage/pallas_call | solution.py:502
  101.5 0.9 copy.12
  102.4 0.7 copy.13
  103.0 0.7 copy.14
Async XLA Ops:
  0.6 50.3 %copy-start = (bf16[768,1024]{1,0:T(8,128)(2,1)S(1)}, bf16[768,1024]{1,0:T(8,128)(2,1)}, u32[]{:S(2)}) copy-start(bf16[768,1024]{1,0:T(8,128)(2,1)} %w_in.1) | copy-start | bytes 4718596
  0.6 50.3 %copy-start.1 = (bf16[512,768]{1,0:T(8,128)(2,1)S(1)}, bf16[512,768]{1,0:T(8,128)(2,1)}, u32[]{:S(2)}) copy-start(bf16[512,768]{1,0:T(8,128)(2,1)} %tokens.1) | copy-start | bytes 2359300
  0.7 50.3 %copy-start.2 = (bf16[512,768]{1,0:T(8,128)(2,1)S(1)}, bf16[512,768]{1,0:T(8,128)(2,1)}, u32[]{:S(2)}) copy-start(bf16[512,768]{1,0:T(8,128)(2,1)} %cotangent.1) | copy-start | bytes 2359300
  0.7 50.3 %copy-start.3 = (s32[512]{0:T(512)S(1)}, s32[512]{0:T(512)}, u32[]{:S(2)}) copy-start(s32[512]{0:T(512)} %param.10) | copy-start | bytes 6148
  0.7 50.3 %copy-start.4 = (s32[512]{0:T(512)S(1)}, s32[512]{0:T(512)}, u32[]{:S(2)}) copy-start(s32[512]{0:T(512)} %param.11) | copy-start | bytes 6148

commit v2 on v1

--- a/solution.py
+++ b/solution.py
@@ -41,16 +41,22 @@
     )
 
 
-CHUNKS = 16
 GROUPS = 2
-PER = CHUNKS // GROUPS
+PER = 8
+CHUNKS = GROUPS * PER
 
 
 def row_kernel(
-    tokens_h, cotangent_h, w_in_h, w_out_h, hid_out,
-    tokens, cotangent, w_in, w_out, snd, prt, acc, rcv, run, hid,
-    pair_s, pair_r, sum_s, sum_r, back_s, back_r, side_s, side_r, out_sem, in_sem,
+    n_batch,
+    tokens_h, cotangent_h, w_in_h, w_out_h, seg_h, keep_h,
+    hid_out, w_tok_out, w_cot_out, weight_out,
+    tokens, cotangent, w_in, w_out, seg, keep,
+    snd, prt, acc, rcv, run, hid,
+    w_tok, w_cot, weights, counts, counts_in,
+    pair_s, pair_r, sum_s, sum_r, back_s, back_r, side_s, side_r,
+    count_s, count_r, out_sem, in_sem, w_sem,
 ):
+    b = lax.axis_index("batch")
     row = lax.axis_index("row")
     core = row % 2
     z = row // 2
@@ -59,12 +65,13 @@
     ahead = {"row": (row + step + 8) % 8}
     behind = {"row": (row - step + 8) % 8}
     partner = {"row": row + 1 - 2 * core}
-    half = acc.shape[3]
-    rows = acc.shape[2]
-    block = PER * rows
+    y_to = ({"batch": (b + 1) % n_batch}, {"batch": (b + n_batch - 1) % n_batch})
+    rows, wide = acc.shape[2], acc.shape[3]
+    toks, width = tokens.shape
+    half = GROUPS * wide
 
     barrier = pltpu.get_barrier_semaphore()
-    for where in (partner, ahead, behind):
+    for where in (partner, ahead, behind) + y_to:
         pl.semaphore_signal(barrier, inc=1, device_id=where, device_id_type=MESH)
 
     def columns(which):
@@ -75,6 +82,8 @@
     loads = [
         pltpu.make_async_copy(src, dst, in_sem.at[i])
         for i, (src, dst) in enumerate((
+            (seg_h, seg),
+            (keep_h, keep),
             (tokens_h, tokens),
             (w_in_h.at[:, other], w_in.at[:, other]),
             (cotangent_h, cotangent),
@@ -86,30 +95,31 @@
     for load in loads:
         load.start()
 
+    loads[0].wait()
+    loads[1].wait()
+    labels = lax.broadcasted_iota(jnp.int32, (SEGS, toks), 0)
+
+    def image_marks():
+        return jnp.where((labels == seg[...]) & (keep[...] == 1), 1.0, 0.0).astype(F32)
+
+    counts[...] = jnp.broadcast_to(
+        jnp.sum(image_marks(), axis=1, keepdims=True), counts.shape
+    )
+
+    def count_copy(d):
+        return remote(counts, counts_in.at[d], count_s.at[d], count_r.at[d], y_to[d])
+
     def pair(g):
         part = pl.ds(g * PER, PER)
         return remote(snd.at[part], prt.at[part], pair_s.at[g], pair_r.at[g], partner)
 
-    def products(cols, g, into, waits=()):
-        toks = pl.ds(g * block, block)
+    def products(which, g, into):
+        cols = pl.ds(pl.multiple_of(which * half + g * wide, wide), wide)
         part = pl.ds(g * PER, PER)
-        for i in waits[:-1]:
-            loads[i].wait()
-        fwd = dot(tokens[toks, :], w_in[:, cols], 1, 0)
-        into[part, 0] = fwd.reshape(PER, rows, half).astype(into.dtype)
-        if waits:
-            loads[waits[-1]].wait()
-        bwd = dot(cotangent[toks, :], w_out[cols, :], 1, 1)
-        into[part, 1] = bwd.reshape(PER, rows, half).astype(into.dtype)
-
-    loads[2].wait()
-    products(other, 0, snd, (0, 1, 3))
-    pl.semaphore_wait(barrier, 3)
-    pair(0).start()
-    products(other, 1, snd)
-    pair(1).start()
-    products(mine, 0, acc, (4, 5))
-    products(mine, 1, acc)
+        fwd = dot(tokens[...], w_in[:, cols], 1, 0)
+        into[part, 0] = fwd.reshape(PER, rows, wide).astype(into.dtype)
+        bwd = dot(cotangent[...], w_out[cols, :], 1, 1)
+        into[part, 1] = bwd.reshape(PER, rows, wide).astype(into.dtype)
 
     def onward(j):
         return remote(run.at[j], rcv.at[j], sum_s.at[j], sum_r.at[j], ahead)
@@ -127,18 +137,60 @@
             hid.at[which, j], hid_out.at[which, j], out_sem.at[which, j]
         )
 
-    for g in range(GROUPS):
-        pair(g).wait_recv()
-
+    def begin(g):
         @pl.when(place == 0)
         def _():
+            pair(g).wait_recv()
+
             @pl.loop(g * PER, (g + 1) * PER)
             def _(j):
                 run[j] = (acc[j] + prt[j].astype(F32)).astype(BF16)
                 onward(j).start()
 
+    for load in loads[2:6]:
+        load.wait()
+    products(1 - core, 0, snd)
+    pl.semaphore_wait(barrier, 5)
+    pair(0).start()
+    count_copy(0).start()
+    count_copy(1).start()
+    products(1 - core, 1, snd)
+    pair(1).start()
+    loads[6].wait()
+    loads[7].wait()
+    products(core, 0, acc)
+    begin(0)
+    products(core, 1, acc)
+    begin(1)
+
+    count_copy(0).wait_recv()
+    count_copy(1).wait_recv()
+    sizes = counts[...] + counts_in[0] + counts_in[1]
+    sizes = jnp.concatenate([sizes, sizes], axis=1)
+    per_token = dot(image_marks(), sizes, 0, 0)
+    weight = jnp.where(
+        per_token > 0.0, jnp.sqrt(IMAGE_MEAN / jnp.maximum(per_token, 1.0)), 0.0
+    )
+    weights[...] = weight
+    span = weight.shape[1]
+    for i in range(width // span):
+        lanes = pl.ds(i * span, span)
+        w_tok[:, lanes] = (tokens[:, lanes].astype(F32) * weight).astype(BF16)
+        w_cot[:, lanes] = (cotangent[:, lanes].astype(F32) * weight).astype(BF16)
+    keeps = [
+        pltpu.make_async_copy(src, dst, w_sem.at[i])
+        for i, (src, dst) in enumerate((
+            (w_tok, w_tok_out), (w_cot, w_cot_out), (weights, weight_out),
+        ))
+    ]
+    for copy in keeps:
+        copy.start()
+
+    for g in range(GROUPS):
         @pl.when((place > 0) & (place < 3))
         def _():
+            pair(g).wait_recv()
+
             @pl.loop(g * PER, (g + 1) * PER)
             def _(j):
                 own = acc[j] + prt[j].astype(F32)
@@ -148,6 +200,8 @@
 
         @pl.when(place == 3)
         def _():
+            pair(g).wait_recv()
+
             @pl.loop(g * PER, (g + 1) * PER)
             def _(j):
                 onward(j).wait_recv()
@@ -180,6 +234,9 @@
 
     for g in range(GROUPS):
         pair(g).wait_send()
+        count_copy(g).wait_send()
+    for copy in keeps:
+        copy.wait()
 
     @pl.loop(0, CHUNKS)
     def _(j):
@@ -200,60 +257,73 @@
             back(j).wait_send()
 
 
-def row_stage(tokens, cotangent, w_in, w_out):
+def row_stage(mesh_shape, tokens, cotangent, w_in, w_out, seg, keep):
     toks, width = tokens.shape
     cols = w_in.shape[1]
-    half = cols // 2
-    rows = toks // CHUNKS
-    slab = (CHUNKS, 2, rows, half)
+    slab = (CHUNKS, 2, toks // PER, cols // 2 // GROUPS)
     dma = pltpu.SemaphoreType.DMA
+    args = [
+        pltpu.with_memory_space_constraint(x, pltpu.MemorySpace.HBM)
+        for x in (tokens, cotangent, w_in, w_out, seg, keep)
+    ]
     return pl.pallas_call(
-        row_kernel,
-        out_shape=jax.ShapeDtypeStruct((2,) + slab, BF16),
-        in_specs=[pl.BlockSpec(memory_space=pltpu.MemorySpace.HBM)] * 4,
-        out_specs=pl.BlockSpec(memory_space=pl.ANY),
+        functools.partial(row_kernel, mesh_shape["batch"]),
+        out_shape=(
+            jax.ShapeDtypeStruct((2,) + slab, BF16),
+            jax.ShapeDtypeStruct((toks, width), BF16),
+            jax.ShapeDtypeStruct((toks, width), BF16),
+            jax.ShapeDtypeStruct((toks, 256), F32),
+        ),
+        in_specs=[pl.BlockSpec(memory_space=pltpu.MemorySpace.HBM)] * 6,
+        out_specs=(pl.BlockSpec(memory_space=pl.ANY),) * 4,
         scratch_shapes=[
             pltpu.VMEM((toks, width), BF16),
             pltpu.VMEM((toks, width), BF16),
             pltpu.VMEM((width, cols), BF16),
             pltpu.VMEM((cols, width), BF16),
+            pltpu.VMEM((1, toks), jnp.int32),
+            pltpu.VMEM((1, toks), jnp.int32),
             pltpu.VMEM(slab, BF16),
             pltpu.VMEM(slab, BF16),
             pltpu.VMEM(slab, F32),
             pltpu.VMEM(slab, BF16),
             pltpu.VMEM(slab, BF16),
             pltpu.VMEM((2,) + slab, BF16),
+            pltpu.VMEM((toks, width), BF16),
+            pltpu.VMEM((toks, width), BF16),
+            pltpu.VMEM((toks, 256), F32),
+            pltpu.VMEM((SEGS, 128), F32),
+            pltpu.VMEM((2, SEGS, 128), F32),
             dma((GROUPS,)), dma((GROUPS,)),
             dma((CHUNKS,)), dma((CHUNKS,)),
             dma((CHUNKS,)), dma((CHUNKS,)),
             dma((CHUNKS,)), dma((CHUNKS,)),
-            dma((2, CHUNKS)),
-            dma((6,)),
+            dma((2,)), dma((2,)),
+            dma((2, CHUNKS)), dma((8,)), dma((3,)),
         ],
         compiler_params=pltpu.CompilerParams(
-            collective_id=0, has_side_effects=True, vmem_limit_bytes=32 << 20
+            collective_id=0, has_side_effects=True, vmem_limit_bytes=36 << 20
         ),
         cost_estimate=pl.CostEstimate(
             flops=4 * toks * width * cols, bytes_accessed=40 << 20, transcendentals=0
         ),
         name="row_stage",
-    )(tokens, cotangent, w_in, w_out)
+    )(*args)
 
 
 def grad_kernel(
     n_batch, n_x, n_z,
-    hid, tokens, cotangent, w_in, seg, keep,
+    hid, w_tok, w_cot, w_in, weights,
     g_tok, g_in, g_out,
-    weighted, grads, y_first, y_rest, part, x_first, x_last, z_send, z_recv, total,
-    counts, counts_in,
-    count_s, count_r, y_s, y_r, x_s, x_r, z_s, z_r, zg_s, zg_r, xg_s, xg_r, out_sem,
+    grads, y_first, y_rest, part, x_first, x_last, z_send, z_recv, total,
+    y_s, y_r, x_s, x_r, z_s, z_r, zg_s, zg_r, xg_s, xg_r, out_sem,
 ):
     b = lax.axis_index("batch")
     col = lax.axis_index("col")
     xi = col // n_z
     q = col % n_z
-    half = hid.shape[4]
-    toks = tokens.shape[0]
+    wide = hid.shape[4]
+    toks = w_tok.shape[0]
     third = part.shape[2]
     piece = grads.shape[2]
     split = piece // 2
@@ -275,39 +345,14 @@
     for where in y_to + x_to + z_to:
         pl.semaphore_signal(barrier, inc=1, device_id=where, device_id_type=MESH)
 
-    labels = lax.broadcasted_iota(jnp.int32, (SEGS, toks), 0)
-    marks = jnp.where((labels == seg[...]) & (keep[...] == 1), 1.0, 0.0).astype(F32)
-    counts[...] = jnp.broadcast_to(
-        jnp.sum(marks, axis=1, keepdims=True), counts.shape
-    )
-    pl.semaphore_wait(barrier, 6)
-
-    def count_copy(d):
-        return remote(counts, counts_in.at[d], count_s.at[d], count_r.at[d], y_to[d])
-
-    count_copy(0).start()
-    count_copy(1).start()
-
-    def hidden(h, a):
-        return hid[h, :, a].reshape(toks, half)
-
-    raw = []
-    for i in range(3):
-        rows = pl.ds(i * third, third)
-        raw.append(
-            dot(hidden(0, 1), w_in[rows, 0:half], 1, 1)
-            + dot(hidden(1, 1), w_in[rows, half:2 * half], 1, 1)
-        )
-    count_copy(0).wait_recv()
-    count_copy(1).wait_recv()
-    sizes = counts[...] + counts_in[0] + counts_in[1]
-    sizes = jnp.concatenate([sizes, sizes], axis=1)
-    per_token = dot(marks, sizes, 0, 0)
-    weight = jnp.where(
-        per_token > 0.0, jnp.sqrt(IMAGE_MEAN / jnp.maximum(per_token, 1.0)), 0.0
-    )
-    for i in range(3):
-        part[i] = (raw[i] * weight).astype(BF16)
+    blocks = [(h, g) for h in range(2) for g in range(GROUPS)]
+
+    def hidden(h, g, a):
+        return hid[h, g * PER:(g + 1) * PER, a].reshape(toks, wide)
+
+    def place(h, g):
+        first = (h * GROUPS + g) * wide
+        return slice(first, first + wide)
 
     def rows_of(ref, owner, start, size):
         first = pl.multiple_of(owner * own_rows + start, size)
@@ -326,10 +371,6 @@
             dst = x_last.at[u, d]
         return remote(src, dst, x_s.at[u, s, d], x_r.at[u, s, d], x_to[d])
 
-    for u in range(2):
-        x_sum(u, 0, 0).start()
-        x_sum(u, 0, 1).start()
-
     def y_owner(s, d):
         shift = 4 - s
         return (b + shift) % n_batch if d == 0 else (b + n_batch - shift) % n_batch
@@ -344,16 +385,24 @@
         return remote(src, dst, y_s.at[a, s, d], y_r.at[a, s, d], y_to[d])
 
     def products(a, source):
-        for i in range(3):
-            lanes = pl.ds(i * third, third)
-            weighted[:, lanes] = (source[:, lanes].astype(F32) * weight).astype(BF16)
-        for h in range(2):
-            block = dot(weighted[...], hidden(h, 1 - a), 0, 0)
-            grads[a, :, :, h * half:(h + 1) * half] = block.reshape(
-                n_batch, piece, half
-            ).astype(BF16)
+        for h, g in blocks:
+            block = dot(source[...], hidden(h, g, 1 - a), 0, 0)
+            grads[a, :, :, place(h, g)] = block.reshape(n_batch, piece, wide).astype(BF16)
+
+    def y_begin(a):
         y_sum(a, 0, 0).start()
         y_sum(a, 0, 1).start()
+
+    def input_products():
+        for i in range(3):
+            rows = pl.ds(i * third, third)
+            raw = sum(
+                dot(hidden(h, g, 1), w_in[rows, place(h, g)], 1, 1) for h, g in blocks
+            )
+            part[i] = (raw * weights[...]).astype(BF16)
+        for u in range(2):
+            x_sum(u, 0, 0).start()
+            x_sum(u, 0, 1).start()
 
     def y_onward(a, s):
         for d in range(2):
@@ -448,10 +497,14 @@
             total.at[i], g_tok.at[:, pl.ds(i * third, third)], out_sem.at[i]
         )
 
-    products(1, cotangent)
+    products(1, w_cot)
+    pl.semaphore_wait(barrier, 6)
+    y_begin(1)
+    input_products()
+    products(0, w_tok)
+    y_begin(0)
     x_onward(0)
     x_onward(1)
-    products(0, tokens)
     z_scatter(0)
     y_onward(1, 1)
     z_scatter(1)
@@ -475,7 +528,6 @@
     y_finish(0, g_in)
 
     for d in range(2):
-        count_copy(d).wait_send()
         for u in range(2):
             z_sum(u, d).wait_send()
             z_give(u, d).wait_send()
@@ -489,10 +541,10 @@
         save(i).wait()
 
 
-def grad_stage(mesh_shape, hid, tokens, cotangent, w_in, seg, keep):
+def grad_stage(mesh_shape, hid, w_tok, w_cot, w_in, weights):
     n_batch = mesh_shape["batch"]
     n_x, n_z = 4, mesh_shape["col"] // 4
-    toks, width = tokens.shape
+    toks, width = w_tok.shape
     cols = w_in.shape[1]
     third = width // 3
     piece = width // n_batch
@@ -506,10 +558,9 @@
             jax.ShapeDtypeStruct((piece, cols), BF16),
             jax.ShapeDtypeStruct((piece, cols), BF16),
         ),
-        in_specs=[vmem] * 6,
+        in_specs=[vmem] * 5,
         out_specs=(pl.BlockSpec(memory_space=pl.ANY), vmem, vmem),
         scratch_shapes=[
-            pltpu.VMEM((toks, width), BF16),
             pltpu.VMEM((2, n_batch, piece, cols), BF16),
             pltpu.VMEM((2, 2, piece // 2, cols), BF16),
             pltpu.VMEM((2, 2, 3, piece, cols), BF16),
@@ -519,9 +570,6 @@
             pltpu.VMEM((2, 3, own // 2, third), BF16),
             pltpu.VMEM((2, 2, own // 2, third), BF16),
             pltpu.VMEM((3, toks, third), BF16),
-            pltpu.VMEM((SEGS, 128), F32),
-            pltpu.VMEM((2, SEGS, 128), F32),
-            dma((2,)), dma((2,)),
             dma((2, 4, 2)), dma((2, 4, 2)),
             dma((2, 2, 2)), dma((2, 2, 2)),
             dma((2, 2)), dma((2, 2)),
@@ -530,23 +578,47 @@
             dma((3,)),
         ],
         compiler_params=pltpu.CompilerParams(
-            collective_id=1, has_side_effects=True, vmem_limit_bytes=40 << 20
+            collective_id=1, has_side_effects=True, vmem_limit_bytes=36 << 20
         ),
         cost_estimate=pl.CostEstimate(
             flops=6 * toks * width * cols, bytes_accessed=40 << 20, transcendentals=0
         ),
         name="grad_stage",
-    )(hid, tokens, cotangent, w_in, seg, keep)
+    )(hid, w_tok, w_cot, w_in, weights)
+
+
+def publish_kernel(*refs):
+    count = (len(refs) - 1) // 2
+    copies = [
+        pltpu.make_async_copy(refs[i], refs[count + i], refs[-1].at[i])
+        for i in range(count)
+    ]
+    for copy in copies:
+        copy.start()
+    for copy in copies:
+        copy.wait()
+
+
+def publish(*arrays):
+    anywhere = pl.BlockSpec(memory_space=pl.ANY)
+    return pl.pallas_call(
+        publish_kernel,
+        out_shape=tuple(jax.ShapeDtypeStruct(x.shape, x.dtype) for x in arrays),
+        in_specs=[anywhere] * len(arrays),
+        out_specs=(anywhere,) * len(arrays),
+        scratch_shapes=[pltpu.SemaphoreType.DMA((len(arrays),))],
+        compiler_params=pltpu.CompilerParams(vmem_limit_bytes=8 << 20),
+        name="publish",
+    )(*arrays)
 
 
 def per_device(mesh_shape, tokens, cotangent, weight_in, weight_out, segment_ids, keep_mask):
-    hid = row_stage(*(
-        pltpu.with_memory_space_constraint(x, pltpu.MemorySpace.HBM)
-        for x in (tokens, cotangent, weight_in, weight_out)
-    ))
-    grad_tokens, grad_in, grad_out = grad_stage(
-        mesh_shape, hid, tokens, cotangent, weight_in,
+    hid, w_tok, w_cot, weights = row_stage(
+        mesh_shape, tokens, cotangent, weight_in, weight_out,
         segment_ids[None, :], keep_mask[None, :],
+    )
+    grad_tokens, grad_in, grad_out = publish(
+        *grad_stage(mesh_shape, hid, w_tok, w_cot, weight_in, weights)
     )
     return (grad_tokens, grad_in, grad_out.T)
 

time: 104 us -> 97.7 us (0.939)
  the two profiles are of different devices: /device:TPU:192 before, /device:TPU:1 now
where the time goes in v2:
time: 97.7 us; the launch traced here: 96.5 us
  Pallas kernels  95.8 us (98%)
    pallas_call x1, Pallas kernels, row_stage(): pl.pallas_call(functools.partial(row_kernel, mesh_shape['batch']), out_sh...  51.8 us
    pallas_call x1, Pallas kernels, grad_stage(): pl.pallas_call(functools.partial(grad_kernel, n_batch, n_x, n_z), out_sha...  43 us

profile of v2, /device:TPU:1, one launch (start us, length us, event | category | flops | bytes accessed | tf_op | source)
XLA Modules:
  0.0 96.5 jit_solution(6651120429565424164)
XLA Ops:
  0.6 0.0 copy-start
  0.6 51.8 %row_stage.1 = (bf16[2,16,2,64,256]{4,3,2,1,0:T(8,128)(2,1)S(1)}, bf16[512,768]{1,0:T(8,128)(2,1)S(1)}, bf16[512,768]{1,0:T(8,128)(2,1)S(1)}, f32[512,256]{1,0:T(8,128)S(1)}) custom-call(bf16[512,768]{1,0:T(8,128)(2,1)} %tokens_h.1, bf16[512,768]{1,0:T(8,128)(2,1)} %cotangent_h.1, bf16[768,1024]{1,0:T(8,128)(2,1)} %w_in.1, bf16[1024,768]{1,0:T(8,128)(2,1)} %w_out_h.1, ...), custom_call_target="tpu_custom_call" | custom-call | flops 1610612736 | bytes 41943040 | tf_op jit(solution)/shard_map/row_stage/pallas_call | solution.py:269
  52.4 0.0 copy-done
  52.4 43.0 %grad_stage.1 = (bf16[512,768]{1,0:T(8,128)(2,1)S(1)}, bf16[96,1024]{1,0:T(8,128)(2,1)S(1)}, bf16[96,1024]{1,0:T(8,128)(2,1)S(1)}) custom-call(bf16[2,16,2,64,256]{4,3,2,1,0:T(8,128)(2,1)S(1)} %get-tuple-element.13.hid, bf16[512,768]{1,0:T(8,128)(2,1)S(1)} %get-tuple-element.14.w_tok, bf16[512,768]{1,0:T(8,128)(2,1)S(1)} %get-tuple-element.15.w_cot, ...), custom_call_target="tpu_custom_call" | custom-call | flops 2415919104 | bytes 41943040 | tf_op jit(solution)/shard_map/grad_stage/pallas_call | solution.py:554
  95.4 1.0 %publish.1 = (bf16[512,768]{1,0:T(8,128)(2,1)}, bf16[96,1024]{1,0:T(8,128)(2,1)}, bf16[96,1024]{1,0:T(8,128)(2,1)}) custom-call(bf16[512,768]{1,0:T(8,128)(2,1)S(1)} %get-tuple-element.17.refs_0_, bf16[96,1024]{1,0:T(8,128)(2,1)S(1)} %get-tuple-element.18.refs_1_, bf16[96,1024]{1,0:T(8,128)(2,1)S(1)} %get-tuple-element.19.refs_2_), custom_call_target="tpu_custom_call" | custom-call | tf_op jit(solution)/shard_map/publish/pallas_call | solution.py:604
Async XLA Ops:
  0.6 51.8 %copy-start = (bf16[768,1024]{1,0:T(8,128)(2,1)S(1)}, bf16[768,1024]{1,0:T(8,128)(2,1)}, u32[]{:S(2)}) copy-start(bf16[768,1024]{1,0:T(8,128)(2,1)} %w_in.1) | copy-start | bytes 4718596

commit v3 on v2

--- a/solution.py
+++ b/solution.py
@@ -186,46 +186,65 @@
     for copy in keeps:
         copy.start()
 
-    for g in range(GROUPS):
-        @pl.when((place > 0) & (place < 3))
-        def _():
+    def sum_step(j):
+        own = acc[j] + prt[j].astype(F32)
+        onward(j).wait_recv()
+        run[j] = (own + rcv[j].astype(F32)).astype(BF16)
+        onward(j).start()
+
+    def finish_step(j):
+        onward(j).wait_recv()
+        pre = acc[j, 0] + prt[j, 0].astype(F32) + rcv[j, 0].astype(F32)
+        grad = acc[j, 1] + prt[j, 1].astype(F32) + rcv[j, 1].astype(F32)
+        act, slopes = gelu_parts(pre)
+        hid[core, j, 0] = act.astype(BF16)
+        hid[core, j, 1] = (grad * slopes).astype(BF16)
+        back(j).start()
+        side(j, core).start()
+        save(j, core).start()
+
+    def back_step(j, further):
+        back(j).wait_recv()
+        if further:
+            back(j).start()
+        side(j, core).start()
+        save(j, core).start()
+
+    def relay(lag):
+        @pl.loop(0, lag)
+        def _(j):
+            sum_step(j)
+
+        @pl.loop(lag, CHUNKS)
+        def _(j):
+            sum_step(j)
+            back_step(j - lag, True)
+
+        @pl.loop(CHUNKS - lag, CHUNKS)
+        def _(j):
+            back_step(j, True)
+
+    @pl.when(place > 0)
+    def _():
+        for g in range(GROUPS):
             pair(g).wait_recv()
 
-            @pl.loop(g * PER, (g + 1) * PER)
-            def _(j):
-                own = acc[j] + prt[j].astype(F32)
-                onward(j).wait_recv()
-                run[j] = (own + rcv[j].astype(F32)).astype(BF16)
-                onward(j).start()
-
-        @pl.when(place == 3)
-        def _():
-            pair(g).wait_recv()
-
-            @pl.loop(g * PER, (g + 1) * PER)
-            def _(j):
-                onward(j).wait_recv()
-                pre = acc[j, 0] + prt[j, 0].astype(F32) + rcv[j, 0].astype(F32)
-                grad = acc[j, 1] + prt[j, 1].astype(F32) + rcv[j, 1].astype(F32)
-                act, slopes = gelu_parts(pre)
-                hid[core, j, 0] = act.astype(BF16)
-                hid[core, j, 1] = (grad * slopes).astype(BF16)
-                back(j).start()
-                side(j, core).start()
-                save(j, core).start()
-
-    @pl.when(place < 3)
+    @pl.when(place == 0)
     def _():
         @pl.loop(0, CHUNKS)
         def _(j):
-            back(j).wait_recv()
-
-            @pl.when(place > 0)
-            def _():
-                back(j).start()
-
-            side(j, core).start()
-            save(j, core).start()
+            back_step(j, False)
+
+    for spot, lag in ((1, 12), (2, 8)):
+        @pl.when(place == spot)
+        def _():
+            relay(lag)
+
+    @pl.when(place == 3)
+    def _():
+        @pl.loop(0, CHUNKS)
+        def _(j):
+            finish_step(j)
 
     @pl.loop(0, CHUNKS)
     def _(j):

time: 97.7 us -> 96.3 us (0.986)
  Pallas kernels: 95.8 us -> 94.7 us
    pallas_call x1, Pallas kernels: 51.8 us -> 50.4 us  [row_stage(): pl.pallas_call(functools.partial(row_kernel, mesh_shape['batch']), out_sh...]
where the time goes in v3:
time: 96.3 us; the launch traced here: 95.3 us
  Pallas kernels  94.7 us (98%)
    pallas_call x1, Pallas kernels, row_stage(): pl.pallas_call(functools.partial(row_kernel, mesh_shape['batch']), out_sh...  50.4 us
    pallas_call x1, Pallas kernels, grad_stage(): pl.pallas_call(functools.partial(grad_kernel, n_batch, n_x, n_z), out_sha...  43.2 us

profile of v3, /device:TPU:1, one launch (start us, length us, event | category | flops | bytes accessed | tf_op | source)
XLA Modules:
  0.0 95.3 jit_solution(9113421769392144806)
XLA Ops:
  0.6 0.0 copy-start
  0.6 50.4 %row_stage.1 = (bf16[2,16,2,64,256]{4,3,2,1,0:T(8,128)(2,1)S(1)}, bf16[512,768]{1,0:T(8,128)(2,1)S(1)}, bf16[512,768]{1,0:T(8,128)(2,1)S(1)}, f32[512,256]{1,0:T(8,128)S(1)}) custom-call(bf16[512,768]{1,0:T(8,128)(2,1)} %tokens_h.1, bf16[512,768]{1,0:T(8,128)(2,1)} %cotangent_h.1, bf16[768,1024]{1,0:T(8,128)(2,1)} %w_in.1, bf16[1024,768]{1,0:T(8,128)(2,1)} %w_out_h.1, ...), custom_call_target="tpu_custom_call" | custom-call | flops 1610612736 | bytes 41943040 | tf_op jit(solution)/shard_map/row_stage/pallas_call | solution.py:288
  51.1 0.0 copy-done
  51.1 43.2 %grad_stage.1 = (bf16[512,768]{1,0:T(8,128)(2,1)S(1)}, bf16[96,1024]{1,0:T(8,128)(2,1)S(1)}, bf16[96,1024]{1,0:T(8,128)(2,1)S(1)}) custom-call(bf16[2,16,2,64,256]{4,3,2,1,0:T(8,128)(2,1)S(1)} %get-tuple-element.13.hid, bf16[512,768]{1,0:T(8,128)(2,1)S(1)} %get-tuple-element.14.w_tok, bf16[512,768]{1,0:T(8,128)(2,1)S(1)} %get-tuple-element.15.w_cot, ...), custom_call_target="tpu_custom_call" | custom-call | flops 2415919104 | bytes 41943040 | tf_op jit(solution)/shard_map/grad_stage/pallas_call | solution.py:573
  94.3 1.0 %publish.1 = (bf16[512,768]{1,0:T(8,128)(2,1)}, bf16[96,1024]{1,0:T(8,128)(2,1)}, bf16[96,1024]{1,0:T(8,128)(2,1)}) custom-call(bf16[512,768]{1,0:T(8,128)(2,1)S(1)} %get-tuple-element.17.refs_0_, bf16[96,1024]{1,0:T(8,128)(2,1)S(1)} %get-tuple-element.18.refs_1_, bf16[96,1024]{1,0:T(8,128)(2,1)S(1)} %get-tuple-element.19.refs_2_), custom_call_target="tpu_custom_call" | custom-call | tf_op jit(solution)/shard_map/publish/pallas_call | solution.py:623
Async XLA Ops:
  0.6 50.4 %copy-start = (bf16[768,1024]{1,0:T(8,128)(2,1)S(1)}, bf16[768,1024]{1,0:T(8,128)(2,1)}, u32[]{:S(2)}) copy-start(bf16[768,1024]{1,0:T(8,128)(2,1)} %w_in.1) | copy-start | bytes 4718596

commit v4 on v3

--- a/solution.py
+++ b/solution.py
@@ -235,7 +235,7 @@
         def _(j):
             back_step(j, False)
 
-    for spot, lag in ((1, 12), (2, 8)):
+    for spot, lag in ((1, 15), (2, 10)):
         @pl.when(place == spot)
         def _():
             relay(lag)
@@ -419,6 +419,8 @@
                 dot(hidden(h, g, 1), w_in[rows, place(h, g)], 1, 1) for h, g in blocks
             )
             part[i] = (raw * weights[...]).astype(BF16)
+
+    def x_begin():
         for u in range(2):
             x_sum(u, 0, 0).start()
             x_sum(u, 0, 1).start()
@@ -516,35 +518,36 @@
             total.at[i], g_tok.at[:, pl.ds(i * third, third)], out_sem.at[i]
         )
 
-    products(1, w_cot)
+    input_products()
     pl.semaphore_wait(barrier, 6)
-    y_begin(1)
-    input_products()
+    x_begin()
     products(0, w_tok)
     y_begin(0)
+    products(1, w_cot)
+    y_begin(1)
     x_onward(0)
     x_onward(1)
+    y_onward(0, 1)
     z_scatter(0)
     y_onward(1, 1)
     z_scatter(1)
-    y_onward(0, 1)
+    y_onward(0, 2)
     z_gather(0)
     y_onward(1, 2)
     z_gather(1)
-    y_onward(0, 2)
+    y_onward(0, 3)
     x_gather(0)
     y_onward(1, 3)
     x_gather(1)
     x_forward(0)
-    y_onward(0, 3)
     x_forward(1)
+    y_finish(0, g_in)
     y_finish(1, g_out)
     for u in range(2):
         x_give(u, 1, 0).wait_recv()
         x_give(u, 1, 1).wait_recv()
     for i in range(3):
         save(i).start()
-    y_finish(0, g_in)
 
     for d in range(2):
         for u in range(2):

time: 96.3 us -> 93.6 us (0.972)
  Pallas kernels: 94.7 us -> 92.4 us
    pallas_call x1, Pallas kernels: 43.2 us -> 41.8 us  [grad_stage(): pl.pallas_call(functools.partial(grad_kernel, n_batch, n_x, n_z), out_sha...]
where the time goes in v4:
time: 93.6 us; the launch traced here: 93.1 us
  Pallas kernels  92.4 us (99%)
    pallas_call x1, Pallas kernels, row_stage(): pl.pallas_call(functools.partial(row_kernel, mesh_shape['batch']), out_sh...  49.6 us
    pallas_call x1, Pallas kernels, grad_stage(): pl.pallas_call(functools.partial(grad_kernel, n_batch, n_x, n_z), out_sha...  41.8 us

profile of v4, /device:TPU:1, one launch (start us, length us, event | category | flops | bytes accessed | tf_op | source)
XLA Modules:
  0.0 93.1 jit_solution(10261675346924597858)
XLA Ops:
  0.6 0.0 copy-start
  0.6 49.6 %row_stage.1 = (bf16[2,16,2,64,256]{4,3,2,1,0:T(8,128)(2,1)S(1)}, bf16[512,768]{1,0:T(8,128)(2,1)S(1)}, bf16[512,768]{1,0:T(8,128)(2,1)S(1)}, f32[512,256]{1,0:T(8,128)S(1)}) custom-call(bf16[512,768]{1,0:T(8,128)(2,1)} %tokens_h.1, bf16[512,768]{1,0:T(8,128)(2,1)} %cotangent_h.1, bf16[768,1024]{1,0:T(8,128)(2,1)} %w_in.1, bf16[1024,768]{1,0:T(8,128)(2,1)} %w_out_h.1, ...), custom_call_target="tpu_custom_call" | custom-call | flops 1610612736 | bytes 41943040 | tf_op jit(solution)/shard_map/row_stage/pallas_call | solution.py:288
  50.2 0.0 copy-done
  50.3 41.8 %grad_stage.1 = (bf16[512,768]{1,0:T(8,128)(2,1)S(1)}, bf16[96,1024]{1,0:T(8,128)(2,1)S(1)}, bf16[96,1024]{1,0:T(8,128)(2,1)S(1)}) custom-call(bf16[2,16,2,64,256]{4,3,2,1,0:T(8,128)(2,1)S(1)} %get-tuple-element.13.hid, bf16[512,768]{1,0:T(8,128)(2,1)S(1)} %get-tuple-element.14.w_tok, bf16[512,768]{1,0:T(8,128)(2,1)S(1)} %get-tuple-element.15.w_cot, ...), custom_call_target="tpu_custom_call" | custom-call | flops 2415919104 | bytes 41943040 | tf_op jit(solution)/shard_map/grad_stage/pallas_call | solution.py:576
  92.0 1.0 %publish.1 = (bf16[512,768]{1,0:T(8,128)(2,1)}, bf16[96,1024]{1,0:T(8,128)(2,1)}, bf16[96,1024]{1,0:T(8,128)(2,1)}) custom-call(bf16[512,768]{1,0:T(8,128)(2,1)S(1)} %get-tuple-element.17.refs_0_, bf16[96,1024]{1,0:T(8,128)(2,1)S(1)} %get-tuple-element.18.refs_1_, bf16[96,1024]{1,0:T(8,128)(2,1)S(1)} %get-tuple-element.19.refs_2_), custom_call_target="tpu_custom_call" | custom-call | tf_op jit(solution)/shard_map/publish/pallas_call | solution.py:626
Async XLA Ops:
  0.6 49.6 %copy-start = (bf16[768,1024]{1,0:T(8,128)(2,1)S(1)}, bf16[768,1024]{1,0:T(8,128)(2,1)}, u32[]{:S(2)}) copy-start(bf16[768,1024]{1,0:T(8,128)(2,1)} %w_in.1) | copy-start | bytes 4718596

commit v5 on v4

--- a/solution.py
+++ b/solution.py
@@ -330,6 +330,9 @@
     )(*args)
 
 
+STREAMS = 4
+
+
 def grad_kernel(
     n_batch, n_x, n_z,
     hid, w_tok, w_cot, w_in, weights,
@@ -344,11 +347,11 @@
     wide = hid.shape[4]
     toks = w_tok.shape[0]
     third = part.shape[2]
-    piece = grads.shape[2]
+    piece = grads.shape[3]
     split = piece // 2
     own_rows = toks // n_x
-    own_half = own_rows // 2
-    own_split = own_half // 2
+    own_part = own_rows // STREAMS
+    own_split = own_part // 2
 
     y_next = {"batch": (b + 1) % n_batch}
     y_prev = {"batch": (b + n_batch - 1) % n_batch}
@@ -381,12 +384,12 @@
     x_near = ((xi + 1) % n_x, (xi + n_x - 1) % n_x)
 
     def x_sum(u, s, d):
-        start = u * own_half
+        start = u * own_part
         if s == 0:
             src = rows_of(part, x_far, start + d * own_split, own_split)
             dst = x_first.at[u, d]
         else:
-            src = rows_of(part, x_near[d], start, own_half)
+            src = rows_of(part, x_near[d], start, own_part)
             dst = x_last.at[u, d]
         return remote(src, dst, x_s.at[u, s, d], x_r.at[u, s, d], x_to[d])
 
@@ -394,23 +397,27 @@
         shift = 4 - s
         return (b + shift) % n_batch if d == 0 else (b + n_batch - shift) % n_batch
 
-    def y_sum(a, s, d):
-        src = grads.at[a, y_owner(s, d)]
+    def y_sum(a, h, s, d):
+        src = grads.at[a, h, y_owner(s, d)]
         if s == 0:
             src = src.at[pl.ds(d * split, split), :]
-            dst = y_first.at[a, d]
+            dst = y_first.at[a, h, d]
         else:
-            dst = y_rest.at[a, d, s - 1]
-        return remote(src, dst, y_s.at[a, s, d], y_r.at[a, s, d], y_to[d])
-
-    def products(a, source):
-        for h, g in blocks:
-            block = dot(source[...], hidden(h, g, 1 - a), 0, 0)
-            grads[a, :, :, place(h, g)] = block.reshape(n_batch, piece, wide).astype(BF16)
-
-    def y_begin(a):
-        y_sum(a, 0, 0).start()
-        y_sum(a, 0, 1).start()
+            dst = y_rest.at[a, h, d, s - 1]
+        return remote(src, dst, y_s.at[a, h, s, d], y_r.at[a, h, s, d], y_to[d])
+
+    sources = (w_tok, w_cot)
+
+    def products(a, h):
+        for g in range(GROUPS):
+            block = dot(sources[a][...], hidden(h, g, 1 - a), 0, 0)
+            grads[a, h, :, :, g * wide:(g + 1) * wide] = block.reshape(
+                n_batch, piece, wide
+            ).astype(BF16)
+
+    def y_begin(a, h):
+        y_sum(a, h, 0, 0).start()
+        y_sum(a, h, 0, 1).start()
 
     def input_products():
         for i in range(3):
@@ -421,38 +428,42 @@
             part[i] = (raw * weights[...]).astype(BF16)
 
     def x_begin():
-        for u in range(2):
+        for u in range(STREAMS):
             x_sum(u, 0, 0).start()
             x_sum(u, 0, 1).start()
 
-    def y_onward(a, s):
+    def y_onward(a, h, s):
         for d in range(2):
-            y_sum(a, s - 1, d).wait_recv()
+            y_sum(a, h, s - 1, d).wait_recv()
             owner = y_owner(s, d)
             if s == 1:
                 lines = pl.ds(d * split, split)
-                grads[a, owner, lines, :] = (
-                    grads[a, owner, lines, :].astype(F32) + y_first[a, d].astype(F32)
+                grads[a, h, owner, lines, :] = (
+                    grads[a, h, owner, lines, :].astype(F32)
+                    + y_first[a, h, d].astype(F32)
                 ).astype(BF16)
             else:
-                grads[a, owner] = (
-                    grads[a, owner].astype(F32) + y_rest[a, d, s - 2].astype(F32)
+                grads[a, h, owner] = (
+                    grads[a, h, owner].astype(F32) + y_rest[a, h, d, s - 2].astype(F32)
                 ).astype(BF16)
-            y_sum(a, s, d).start()
-
-    def y_finish(a, out):
-        y_sum(a, 3, 0).wait_recv()
-        y_sum(a, 3, 1).wait_recv()
-        out[...] = (
-            grads[a, b].astype(F32)
-            + y_rest[a, 0, 2].astype(F32)
-            + y_rest[a, 1, 2].astype(F32)
+            y_sum(a, h, s, d).start()
+
+    outs = (g_in, g_out)
+
+    def y_finish(a, h):
+        y_sum(a, h, 3, 0).wait_recv()
+        y_sum(a, h, 3, 1).wait_recv()
+        cols = GROUPS * wide
+        outs[a][:, h * cols:(h + 1) * cols] = (
+            grads[a, h, b].astype(F32)
+            + y_rest[a, h, 0, 2].astype(F32)
+            + y_rest[a, h, 1, 2].astype(F32)
         ).astype(BF16)
 
     def x_onward(u):
         for d in range(2):
             x_sum(u, 0, d).wait_recv()
-            first = x_near[d] * own_rows + u * own_half + d * own_split
+            first = x_near[d] * own_rows + u * own_part + d * own_split
             lines = pl.ds(pl.multiple_of(first, own_split), own_split)
             part[:, lines, :] = (
                 part[:, lines, :].astype(F32) + x_first[u, d].astype(F32)
@@ -466,7 +477,7 @@
         )
 
     def mine(u):
-        return pl.ds(pl.multiple_of(xi * own_rows + u * own_half, own_half), own_half)
+        return pl.ds(pl.multiple_of(xi * own_rows + u * own_part, own_part), own_part)
 
     def z_scatter(u):
         x_sum(u, 1, 0).wait_recv()
@@ -495,9 +506,9 @@
         z_give(u, 1).start()
 
     def x_give(u, s, d):
-        start = u * own_half
+        start = u * own_part
         if s == 0:
-            spot = rows_of(total, xi, start, own_half)
+            spot = rows_of(total, xi, start, own_part)
         else:
             spot = rows_of(total, x_near[1 - d], start + d * own_split, own_split)
         return remote(spot, spot, xg_s.at[u, s, d], xg_r.at[u, s, d], x_to[d])
@@ -518,39 +529,66 @@
             total.at[i], g_tok.at[:, pl.ds(i * third, third)], out_sem.at[i]
         )
 
+    def x_finish(u):
+        x_give(u, 1, 0).wait_recv()
+        x_give(u, 1, 1).wait_recv()
+
+    products(0, 0)
     input_products()
     pl.semaphore_wait(barrier, 6)
     x_begin()
-    products(0, w_tok)
-    y_begin(0)
-    products(1, w_cot)
-    y_begin(1)
+    y_begin(0, 0)
+    products(0, 1)
+    y_begin(0, 1)
+    products(1, 0)
+    products(1, 1)
+    y_begin(1, 0)
     x_onward(0)
+    y_begin(1, 1)
     x_onward(1)
-    y_onward(0, 1)
+    y_onward(0, 0, 1)
+    x_onward(2)
+    y_onward(0, 1, 1)
+    x_onward(3)
+    y_onward(1, 1, 1)
+    z_scatter(1)
+    z_scatter(2)
+    y_onward(0, 0, 2)
+    z_scatter(3)
+    y_onward(1, 0, 1)
     z_scatter(0)
-    y_onward(1, 1)
-    z_scatter(1)
-    y_onward(0, 2)
+    y_onward(1, 1, 2)
+    y_onward(0, 1, 2)
+    z_gather(1)
+    z_gather(2)
+    z_gather(3)
     z_gather(0)
-    y_onward(1, 2)
-    z_gather(1)
-    y_onward(0, 3)
+    y_onward(1, 0, 2)
+    y_onward(1, 1, 3)
+    y_onward(0, 0, 3)
+    x_gather(2)
+    y_onward(0, 1, 3)
+    x_gather(1)
+    y_onward(1, 0, 3)
     x_gather(0)
-    y_onward(1, 3)
-    x_gather(1)
+    x_gather(3)
+    x_forward(1)
     x_forward(0)
-    x_forward(1)
-    y_finish(0, g_in)
-    y_finish(1, g_out)
-    for u in range(2):
-        x_give(u, 1, 0).wait_recv()
-        x_give(u, 1, 1).wait_recv()
+    x_forward(2)
+    y_finish(0, 0)
+    y_finish(1, 1)
+    x_forward(3)
+    x_finish(0)
+    y_finish(0, 1)
+    y_finish(1, 0)
+    x_finish(3)
+    x_finish(2)
+    x_finish(1)
     for i in range(3):
         save(i).start()
 
     for d in range(2):
-        for u in range(2):
+        for u in range(STREAMS):
             z_sum(u, d).wait_send()
             z_give(u, d).wait_send()
             for s in range(2):
@@ -558,7 +596,8 @@
                 x_give(u, s, d).wait_send()
         for s in range(4):
             for a in range(2):
-                y_sum(a, s, d).wait_send()
+                for h in range(2):
+                    y_sum(a, h, s, d).wait_send()
     for i in range(3):
         save(i).wait()
 
@@ -570,7 +609,7 @@
     cols = w_in.shape[1]
     third = width // 3
     piece = width // n_batch
-    own = toks // n_x
+    own = toks // n_x // STREAMS
     dma = pltpu.SemaphoreType.DMA
     vmem = pl.BlockSpec(memory_space=pltpu.VMEM)
     return pl.pallas_call(
@@ -583,20 +622,20 @@
         in_specs=[vmem] * 5,
         out_specs=(pl.BlockSpec(memory_space=pl.ANY), vmem, vmem),
         scratch_shapes=[
-            pltpu.VMEM((2, n_batch, piece, cols), BF16),
-            pltpu.VMEM((2, 2, piece // 2, cols), BF16),
-            pltpu.VMEM((2, 2, 3, piece, cols), BF16),
+            pltpu.VMEM((2, 2, n_batch, piece, cols // 2), BF16),
+            pltpu.VMEM((2, 2, 2, piece // 2, cols // 2), BF16),
+            pltpu.VMEM((2, 2, 2, 3, piece, cols // 2), BF16),
             pltpu.VMEM((3, toks, third), BF16),
-            pltpu.VMEM((2, 2, 3, own // 4, third), BF16),
-            pltpu.VMEM((2, 2, 3, own // 2, third), BF16),
-            pltpu.VMEM((2, 3, own // 2, third), BF16),
-            pltpu.VMEM((2, 2, own // 2, third), BF16),
+            pltpu.VMEM((STREAMS, 2, 3, own // 2, third), BF16),
+            pltpu.VMEM((STREAMS, 2, 3, own, third), BF16),
+            pltpu.VMEM((STREAMS, 3, own, third), BF16),
+            pltpu.VMEM((STREAMS, 2, own, third), BF16),
             pltpu.VMEM((3, toks, third), BF16),
-            dma((2, 4, 2)), dma((2, 4, 2)),
-            dma((2, 2, 2)), dma((2, 2, 2)),
-            dma((2, 2)), dma((2, 2)),
-            dma((2, 2)), dma((2, 2)),
-            dma((2, 2, 2)), dma((2, 2, 2)),
+            dma((2, 2, 4, 2)), dma((2, 2, 4, 2)),
+            dma((STREAMS, 2, 2)), dma((STREAMS, 2, 2)),
+            dma((STREAMS, 2)), dma((STREAMS, 2)),
+            dma((STREAMS, 2)), dma((STREAMS, 2)),
+            dma((STREAMS, 2, 2)), dma((STREAMS, 2, 2)),
             dma((3,)),
         ],
         compiler_params=pltpu.CompilerParams(

time: 93.6 us -> 93.4 us (level)
  no operation moved by 1% of the time
where the time goes in v5:
time: 93.4 us; the launch traced here: 93.2 us
  Pallas kernels  92.6 us (99%)
    pallas_call x1, Pallas kernels, row_stage(): pl.pallas_call(functools.partial(row_kernel, mesh_shape['batch']), out_sh...  49.6 us
    pallas_call x1, Pallas kernels, grad_stage(): pl.pallas_call(functools.partial(grad_kernel, n_batch, n_x, n_z), out_sha...  41.9 us

profile of v5, /device:TPU:1, one launch (start us, length us, event | category | flops | bytes accessed | tf_op | source)
XLA Modules:
  0.0 93.2 jit_solution(10313177792483995115)
XLA Ops:
  0.6 0.0 copy-start
  0.6 49.6 %row_stage.1 = (bf16[2,16,2,64,256]{4,3,2,1,0:T(8,128)(2,1)S(1)}, bf16[512,768]{1,0:T(8,128)(2,1)S(1)}, bf16[512,768]{1,0:T(8,128)(2,1)S(1)}, f32[512,256]{1,0:T(8,128)S(1)}) custom-call(bf16[512,768]{1,0:T(8,128)(2,1)} %tokens_h.1, bf16[512,768]{1,0:T(8,128)(2,1)} %cotangent_h.1, bf16[768,1024]{1,0:T(8,128)(2,1)} %w_in.1, bf16[1024,768]{1,0:T(8,128)(2,1)} %w_out_h.1, ...), custom_call_target="tpu_custom_call" | custom-call | flops 1610612736 | bytes 41943040 | tf_op jit(solution)/shard_map/row_stage/pallas_call | solution.py:288
  50.2 0.0 copy-done
  50.3 41.9 %grad_stage.1 = (bf16[512,768]{1,0:T(8,128)(2,1)S(1)}, bf16[96,1024]{1,0:T(8,128)(2,1)S(1)}, bf16[96,1024]{1,0:T(8,128)(2,1)S(1)}) custom-call(bf16[2,16,2,64,256]{4,3,2,1,0:T(8,128)(2,1)S(1)} %get-tuple-element.13.hid, bf16[512,768]{1,0:T(8,128)(2,1)S(1)} %get-tuple-element.14.w_tok, bf16[512,768]{1,0:T(8,128)(2,1)S(1)} %get-tuple-element.15.w_cot, ...), custom_call_target="tpu_custom_call" | custom-call | flops 2415919104 | bytes 41943040 | tf_op jit(solution)/shard_map/grad_stage/pallas_call | solution.py:615
  92.2 1.0 %publish.1 = (bf16[512,768]{1,0:T(8,128)(2,1)}, bf16[96,1024]{1,0:T(8,128)(2,1)}, bf16[96,1024]{1,0:T(8,128)(2,1)}) custom-call(bf16[512,768]{1,0:T(8,128)(2,1)S(1)} %get-tuple-element.17.refs_0_, bf16[96,1024]{1,0:T(8,128)(2,1)S(1)} %get-tuple-element.18.refs_1_, bf16[96,1024]{1,0:T(8,128)(2,1)S(1)} %get-tuple-element.19.refs_2_), custom_call_target="tpu_custom_call" | custom-call | tf_op jit(solution)/shard_map/publish/pallas_call | solution.py:665
Async XLA Ops:
  0.6 49.6 %copy-start = (bf16[768,1024]{1,0:T(8,128)(2,1)S(1)}, bf16[768,1024]{1,0:T(8,128)(2,1)}, u32[]{:S(2)}) copy-start(bf16[768,1024]{1,0:T(8,128)(2,1)} %w_in.1) | copy-start | bytes 4718596

commit v6 on v5

--- a/solution.py
+++ b/solution.py
@@ -42,7 +42,7 @@
 
 
 GROUPS = 2
-PER = 8
+PER = 16
 CHUNKS = GROUPS * PER
 
 
@@ -235,7 +235,7 @@
         def _(j):
             back_step(j, False)
 
-    for spot, lag in ((1, 15), (2, 10)):
+    for spot, lag in ((1, 31), (2, 19)):
         @pl.when(place == spot)
         def _():
             relay(lag)

time: 93.4 us -> 95.5 us (1.022)
  Pallas kernels: 92.6 us -> 94.7 us
    pallas_call x1, Pallas kernels: 49.6 us -> 51.8 us  [row_stage(): pl.pallas_call(functools.partial(row_kernel, mesh_shape['batch']), out_sh...]
where the time goes in v6:
time: 95.5 us; the launch traced here: 95.3 us
  Pallas kernels  94.7 us (99%)
    pallas_call x1, Pallas kernels, row_stage(): pl.pallas_call(functools.partial(row_kernel, mesh_shape['batch']), out_sh...  51.8 us
    pallas_call x1, Pallas kernels, grad_stage(): pl.pallas_call(functools.partial(grad_kernel, n_batch, n_x, n_z), out_sha...  41.9 us

profile of v6, /device:TPU:1, one launch (start us, length us, event | category | flops | bytes accessed | tf_op | source)
XLA Modules:
  0.0 95.3 jit_solution(4882941495067252717)
XLA Ops:
  0.6 0.0 copy-start
  0.6 51.8 %row_stage.1 = (bf16[2,32,2,32,256]{4,3,2,1,0:T(8,128)(2,1)S(1)}, bf16[512,768]{1,0:T(8,128)(2,1)S(1)}, bf16[512,768]{1,0:T(8,128)(2,1)S(1)}, f32[512,256]{1,0:T(8,128)S(1)}) custom-call(bf16[512,768]{1,0:T(8,128)(2,1)} %tokens_h.1, bf16[512,768]{1,0:T(8,128)(2,1)} %cotangent_h.1, bf16[768,1024]{1,0:T(8,128)(2,1)} %w_in.1, bf16[1024,768]{1,0:T(8,128)(2,1)} %w_out_h.1, ...), custom_call_target="tpu_custom_call" | custom-call | flops 1610612736 | bytes 41943040 | tf_op jit(solution)/shard_map/row_stage/pallas_call | solution.py:288
  52.4 0.0 copy-done
  52.4 41.9 %grad_stage.1 = (bf16[512,768]{1,0:T(8,128)(2,1)S(1)}, bf16[96,1024]{1,0:T(8,128)(2,1)S(1)}, bf16[96,1024]{1,0:T(8,128)(2,1)S(1)}) custom-call(bf16[2,32,2,32,256]{4,3,2,1,0:T(8,128)(2,1)S(1)} %get-tuple-element.13.hid, bf16[512,768]{1,0:T(8,128)(2,1)S(1)} %get-tuple-element.14.w_tok, bf16[512,768]{1,0:T(8,128)(2,1)S(1)} %get-tuple-element.15.w_cot, ...), custom_call_target="tpu_custom_call" | custom-call | flops 2415919104 | bytes 41943040 | tf_op jit(solution)/shard_map/grad_stage/pallas_call | solution.py:615
  94.3 1.0 %publish.1 = (bf16[512,768]{1,0:T(8,128)(2,1)}, bf16[96,1024]{1,0:T(8,128)(2,1)}, bf16[96,1024]{1,0:T(8,128)(2,1)}) custom-call(bf16[512,768]{1,0:T(8,128)(2,1)S(1)} %get-tuple-element.17.refs_0_, bf16[96,1024]{1,0:T(8,128)(2,1)S(1)} %get-tuple-element.18.refs_1_, bf16[96,1024]{1,0:T(8,128)(2,1)S(1)} %get-tuple-element.19.refs_2_), custom_call_target="tpu_custom_call" | custom-call | tf_op jit(solution)/shard_map/publish/pallas_call | solution.py:665
Async XLA Ops:
  0.6 51.8 %copy-start = (bf16[768,1024]{1,0:T(8,128)(2,1)S(1)}, bf16[768,1024]{1,0:T(8,128)(2,1)}, u32[]{:S(2)}) copy-start(bf16[768,1024]{1,0:T(8,128)(2,1)} %w_in.1) | copy-start | bytes 4718596
